TPU v7x, 256 devices: a whole 4x4x8 slice. The times are simulated.
256 devices in a mesh: lat: 64 (over x, y_lo, z), coh: 4 (over y_hi, core).
Axes of the slice: x: 4, y: 4 (y_hi: 2, y_lo: 2; y = y_hi * 2 + y_lo), z: 8, core: 2. Of those that a mesh axis runs over, the one named last changes fastest.
Arguments:
- density: float32 [128, 2, 512, 1024], P('coh', None, 'lat'), may hold values from 0.1 to 1
- cotangent: float32 [128, 2, 512, 1024], P('coh', None, 'lat'), may hold values from -0.5 to 1.5
- land_mask: int32 [2, 512, 1024], P(None, 'lat'), may hold values 0 or 1
- east_vel: float32 [2, 512, 1024], P(None, 'lat'), may hold values from -0.4 to 0.4
- north_vel: float32 [2, 512, 1024], P(None, 'lat'), may hold values from -0.4 to 0.4
- diffusion: float32 [2, 512, 1024], P(None, 'lat'), may hold values from 0.02 to 0.2
- age_class: int32 [128], P('coh'), may hold values from 0 to 31, as said below
- mort_rate: float32 [32], replicated, may hold values from 0.05 to 0.5
- crowd_coef: float32 [32], replicated, may hold values from 1 to 4
- mass: float32 [32], replicated, may hold values from 0.5 to 2
- speed: float32 [32], replicated, may hold values from 0.25 to 1
Outputs:
- grad_density: float32 [128, 2, 512, 1024], P('coh', None, 'lat')
- grad_east_vel: float32 [2, 512, 1024], P(None, 'lat', 'coh')
- grad_north_vel: float32 [2, 512, 1024], P(None, 'lat', 'coh')
- grad_diffusion: float32 [2, 512, 1024], P(None, 'lat', 'coh')
Inputs may be any that keep to these rules, and one draw needn't show every extreme that they name: `age_class`: each age class is held by exactly 4 cohorts.
All inputs are finite; a program needn't handle non-finite values. No bound on the sum of `land_mask` on one device may be relied on, other than what follows from the above.
Results may differ from a plain program's by a relative error of at most 0.00014.
Values sent between devices are 32-bit elements; how exact they have to be, the bound alone decides.
No kernel may reach another device: no remote copies, remote signals or barrier semaphores. Data moves between devices by JAX's collectives and lax.ppermute only.
A program may use at most 128 MiB of HBM per device.

v0:
```python
import jax
import jax.numpy as jnp
from jax import lax
from jax.sharding import PartitionSpec as P

COH = 128
STEPS = 2


def extended(value, sides, width):
    for axis, dim in sides:
        devices, length = (lax.axis_size(axis), value.shape[dim])
        up = [(i, (i + 1) % devices) for i in range(devices - 1)]
        down = [(j, i) for i, j in up]
        last = lax.slice_in_dim(value, length - width, length, axis=dim)
        first = lax.slice_in_dim(value, 0, width, axis=dim)
        before = lax.ppermute(last, axis, up)
        after = lax.ppermute(first, axis, down)
        value = jnp.concatenate([before, value, after], axis=dim)
    return value


def lookup(age_class, mort_rate, crowd_coef, mass, speed):
    classes = jnp.arange(mort_rate.shape[0], dtype=jnp.int32)
    onehot = (age_class[:, None] == classes[None, :]).astype(jnp.float32)
    tables = jnp.stack([mort_rate, crowd_coef, mass, speed], axis=1)
    picked = jnp.dot(onehot, tables, precision=lax.Precision.HIGHEST)
    return [picked[:, column][:, None, None, None] for column in range(4)]


def local(
    density,
    cotangent,
    land_mask,
    east_vel,
    north_vel,
    diffusion,
    age_class,
    mort_rate,
    crowd_coef,
    mass,
    speed,
):
    ocean = land_mask.astype(jnp.float32)[None]
    mortal, crowding, weight, swim = lookup(age_class, mort_rate, crowd_coef, mass, speed)
    east_coef = swim * east_vel[None]
    north_coef = swim * north_vel[None]
    kappa = diffusion[None]
    state = density
    saved = []
    for section in range(STEPS):
        crowd = lax.psum(jnp.sum(weight * state, axis=0), "coh") / COH
        survival = jnp.exp(-(mortal + crowding * crowd[None]))
        survived = state * survival
        wet = ocean * survived
        padded = extended(wet, (("lat", 2),), 1)
        north_val = padded[:, :, 2:]
        south_val = padded[:, :, :-2]
        east_val = jnp.roll(wet, -1, axis=3)
        west_val = jnp.roll(wet, 1, axis=3)
        laplace = north_val + south_val + east_val + west_val - 4.0 * wet
        east_diff = 0.5 * (east_val - west_val)
        north_diff = 0.5 * (north_val - south_val)
        state = ocean * (wet + kappa * laplace - east_coef * east_diff - north_coef * north_diff)
        saved.append((survival, survived, laplace, east_diff, north_diff))
    adjoint = cotangent
    shares = None
    for section in reversed(range(STEPS)):
        survival, survived, laplace, east_diff, north_diff = saved[section]
        masked = ocean * adjoint
        grad_east = -jnp.sum(masked * swim * east_diff, axis=0)
        grad_north = -jnp.sum(masked * swim * north_diff, axis=0)
        grad_kappa = jnp.sum(masked * laplace, axis=0)
        pieces = (
            lax.psum_scatter(grad_east, "coh", scatter_dimension=2, tiled=True),
            lax.psum_scatter(grad_north, "coh", scatter_dimension=2, tiled=True),
            lax.psum_scatter(grad_kappa, "coh", scatter_dimension=2, tiled=True),
        )
        shares = pieces if shares is None else jax.tree.map(jnp.add, shares, pieces)
        to_north = (kappa - 0.5 * north_coef) * masked
        to_south = (kappa + 0.5 * north_coef) * masked
        to_east = (kappa - 0.5 * east_coef) * masked
        to_west = (kappa + 0.5 * east_coef) * masked
        stacked = extended(jnp.stack([to_north, to_south]), (("lat", 3),), 1)
        from_below = stacked[0][:, :, :-2]
        from_above = stacked[1][:, :, 2:]
        grad_wet = (
            (1.0 - 4.0 * kappa) * masked
            + jnp.roll(to_east, 1, axis=3)
            + jnp.roll(to_west, -1, axis=3)
            + from_below
            + from_above
        )
        grad_surv = ocean * grad_wet
        pressure = lax.psum(jnp.sum(-crowding * grad_surv * survived, axis=0), "coh")
        adjoint = grad_surv * survival + weight / COH * pressure[None]
    return (adjoint, shares[0], shares[1], shares[2])


def solution(mesh):
    in_specs = (
        P("coh", None, "lat", None),
        P("coh", None, "lat", None),
        P(None, "lat", None),
        P(None, "lat", None),
        P(None, "lat", None),
        P(None, "lat", None),
        P("coh"),
        P(),
        P(),
        P(),
        P(),
    )
    out_specs = (
        P("coh", None, "lat", None),
        P(None, "lat", "coh"),
        P(None, "lat", "coh"),
        P(None, "lat", "coh"),
    )
    return jax.shard_map(local, mesh=mesh, in_specs=in_specs, out_specs=out_specs, check_vma=False)
```

profile of v0, /device:TPU:1, one launch (start us, length us, event | category | flops | bytes accessed | tf_op | source)
XLA Modules:
  0.0 388.2 jit_solution(14787665174152883794)
XLA Ops:
  8.1 3.5 multiply_reduce_fusion.9
  11.7 49.5 %all-reduce.5.cloned.1.call-done = f32[2,8,1024]{2,1,0:T(8,128)} async-done(((f32[2,8,1024]{2,1,0:T(8,128)}), f32[2,8,1024]{2,1,0:T(8,128)}) %all-reduce.5.cloned.1.call-update) | async-done | bytes 65552 | tf_op jit(solution)/shard_map/psum | solution.py:52
  62.0 3.0 fusion.26
  65.0 3.2 collective-permute-start.3
  70.6 3.1 collective-permute-done.3
  73.8 4.0 %collective-permute-done.2 = f32[32,2,1,1024]{3,0,2,1:T(8,128)S(1)} collective-permute-done((f32[32,2,1,1024]{3,0,2,1:T(8,128)S(1)}, f32[32,2,1,1024]{3,0,2,1:T(8,128)S(1)}, u32[]{:S(2)}, u32[]{:S(2)}) %collective-permute-start.2) | collective-permute-done | bytes 262176 | tf_op jit(solution)/shard_map/ppermute | solution.py:18
  77.8 5.9 %fusion.9 = (f32[32,2,8,1024]{3,0,2,1:T(8,128)}, f32[32,2,8,1024]{3,0,2,1:T(8,128)}, f32[1,32,2,8,1024]{4,1,3,2,0:T(8,128)S(1)}, f32[1,32,2,8,1024]{4,1,3,2,0:T(...) fusion(f32[2,8,1024]{2,1,0:T(8,128)S(1)} %copy-done.22, f32[32]{0:T(128)S(1)} %get-tuple-element.58, ...), kind=kLoop, calls=%fused_computation.15 | loop fusion | flops 18333696 | bytes 19726592 | tf_op jit(solution)/shard_map/mul | solution.py:82
  87.4 4.8 %collective-permute-start = (f32[2,32,2,1,1024]{4,1,3,2,0:T(8,128)}, f32[2,32,2,1,1024]{4,1,3,2,0:T(8,128)}, u32[]{:S(2)}, u32[]{:S(2)}) collective-permute-start(f32[2,32,2,1,1024]{4,1,3,2,0:T(8,128)} %get-tuple-element.27), channel_id=1, source_target_pairs={{0,4},{4,8},{8,12},{12,16},{16,20},{20,24},{24,28},{28,32},{32,36}... | collective-permute-start | bytes 1572872 | tf_op jit(solution)/shard_map/ppermute | solution.py:17
  94.4 3.5 slice.170
  99.7 41.5 %all-reduce.7.cloned.1.call-done = f32[2,8,1024]{2,1,0:T(8,128)} async-done(((f32[2,8,1024]{2,1,0:T(8,128)}), f32[2,8,1024]{2,1,0:T(8,128)}) %all-reduce.7.cloned.1.call-update) | async-done | bytes 65552 | tf_op jit(solution)/shard_map/psum | solution.py:52
  142.1 3.1 pad_maximum_fusion
  148.7 4.5 %multiply_reduce_fusion.7 = (f32[2,8,1024]{2,1,0:T(8,128)}, f32[32,2,8,1024]{3,0,2,1:T(8,128)}, f32[32,2,8,1024]{3,0,2,1:T(8,128)S(1)}) fusion(f32[32,2,8,1024]{3,0,2,1:T(8,128)S(1)} %copy-done.13, f32[32]{0:T(128)S(1)} %get-tuple-element.57, f32[2,8,1024]{2,1,0:T(8,128)S(1)} %broadcast_multiply_fusion, f32[32]{0:T(128)S(1)} %get-tuple-element.60, ...), kind=kLoop, calls=%fused_computation.57 | loop fusion | flops 8896512 | bytes 17039744 | tf_op jit(solution)/shard_map/reduce_sum | solution.py:95
  153.3 2.9 fusion.42
  160.3 4.7 %collective-permute-start.7 = (f32[32,2,1,1024]{3,0,2,1:T(8,128)}, f32[32,2,1,1024]{3,0,2,1:T(8,128)}, u32[]{:S(2)}, u32[]{:S(2)}) collective-permute-start(f32[32,2,1,1024]{3,0,2,1:T(8,128)} %get-tuple-element.42), channel_id=1, source_target_pairs={{0,4},{4,8},{8,12},{12,16},{16,20},{20,24},{24,28},{28,32},{32,36}... | collective-permute-start | bytes 786440 | tf_op jit(solution)/shard_map/ppermute | solution.py:17
  165.0 36.8 %all-reduce.9.cloned.1.call-done = f32[2,8,1024]{2,1,0:T(8,128)} async-done(((f32[2,8,1024]{2,1,0:T(8,128)}), f32[2,8,1024]{2,1,0:T(8,128)}) %all-reduce.9.cloned.1.call-update) | async-done | bytes 65552 | tf_op jit(solution)/shard_map/psum | solution.py:95
  201.7 5.3 %multiply_reduce_fusion = (f32[2,8,1024]{2,1,0:T(8,128)}, f32[2,8,1024]{2,1,0:T(8,128)}, f32[2,8,1024]{2,1,0:T(8,128)}, f32[32,2,8,1024]{3,0,2,1:T(8,128)S(1)}) fusion(f32[32,2,8,1024]{3,0,2,1:T(8,128)S(1)} %fusion.26, f32[32,2,8,1023]{3,0,2,1:T(8,128)} %copy-done.6, f32[32,2,8,1]{3,0,2,1:T(8,128)S(1)} %get-tuple-element.53, ...), kind=kLoop, calls=%fused_computation.48 | loop fusion | flops 14106624 | bytes 11403776 | tf_op jit(solution)/shard_map/reduce_sum | solution.py:73
  210.5 4.2 %collective-permute-start.4 = (f32[2,32,2,1,1024]{4,1,3,2,0:T(8,128)S(1)}, f32[2,32,2,1,1024]{4,1,3,2,0:T(8,128)S(1)}, u32[]{:S(2)}, u32[]{:S(2)}) collective-permute-start(f32[2,32,2,1,1024]{4,1,3,2,0:T(8,128)S(1)} %get-tuple-element.25), channel_id=1, source_target_pairs={{0,4},{4,8},{8,12},{12,16},{16,20},{20,24},{24,28},{28,32},{32,36}... | collective-permute-start | bytes 1572872 | tf_op jit(solution)/shard_map/ppermute | solution.py:17
  214.9 4.7 %multiply_reduce_fusion.1 = (f32[2,8,1024]{2,1,0:T(8,128)}, f32[2,8,1024]{2,1,0:T(8,128)}, f32[2,8,1024]{2,1,0:T(8,128)}) fusion(f32[32,2,8,1024]{3,0,2,1:T(8,128)S(1)} %copy-done.1, f32[32,2,8,1023]{3,0,2,1:T(8,128)S(1)} %copy-done.12, f32[32,2,8,1]{3,0,2,1:T(8,128)S(1)} %copy-done.16, f32[32,2,8,1]{3,0,2,1:T(8,128)S(1)} %get-tuple-element.46, ...), kind=kLoop, calls=%fused_computation.49 | loop fusion | flops 10960896 | bytes 9175168 | tf_op jit(solution)/shard_map/reduce_sum | solution.py:73
  219.6 5.1 %collective-permute-done.5 = f32[2,32,2,1,1024]{4,1,3,2,0:T(8,128)S(1)} collective-permute-done((f32[2,32,2,1,1024]{4,1,3,2,0:T(8,128)S(1)}, f32[2,32,2,1,1024]{4,1,3,2,0:T(8,128)S(1)}, u32[]{:S(2)}, u32[]{:S(2)}) %collective-permute-start.5) | collective-permute-done | bytes 524320 | tf_op jit(solution)/shard_map/ppermute | solution.py:18
  228.1 3.6 multiply_reduce_fusion.6
  233.9 45.8 %all-reduce.11.cloned.1.call-done = f32[2,8,1024]{2,1,0:T(8,128)} async-done(((f32[2,8,1024]{2,1,0:T(8,128)}), f32[2,8,1024]{2,1,0:T(8,128)}) %all-reduce.11.cloned.1.call-update) | async-done | bytes 65552 | tf_op jit(solution)/shard_map/psum | solution.py:95
  283.7 29.2 %reduce-scatter.4.cloned.1.call-done = f32[2,8,256]{2,1,0:T(8,128)} async-done(((f32[2,8,1024]{2,1,0:T(8,128)}), f32[2,8,256]{2,1,0:T(8,128)}) %reduce-scatter.4.cloned.1.call-update) | async-done | bytes 16400 | tf_op jit(solution)/shard_map/reduce_scatter | solution.py:75
  312.9 34.2 %reduce-scatter.6.cloned.1.call-done = f32[2,8,256]{2,1,0:T(8,128)} async-done(((f32[2,8,1024]{2,1,0:T(8,128)}), f32[2,8,256]{2,1,0:T(8,128)}) %reduce-scatter.6.cloned.1.call-update) | async-done | bytes 16400 | tf_op jit(solution)/shard_map/reduce_scatter | solution.py:76
  347.0 34.3 %reduce-scatter.8.cloned.1.call-done = f32[2,8,256]{2,1,0:T(8,128)} async-done(((f32[2,8,1024]{2,1,0:T(8,128)}), f32[2,8,256]{2,1,0:T(8,128)}) %reduce-scatter.8.cloned.1.call-update) | async-done | bytes 16400 | tf_op jit(solution)/shard_map/reduce_scatter | solution.py:77
  (119 shorter events, 33.3 us)
Async XLA Ops:
  7.2 54.0 %all-reduce.5.cloned.1.call-start = ((), (), s32[]{:S(2)}) async-start(), calls=%async_computation.3 | async-start | bytes 131072 | tf_op jit(solution)/shard_map/psum | solution.py:52
  11.6 129.6 %all-reduce.7.cloned.1.call-start = ((), (), s32[]{:S(2)}) async-start(), calls=%async_computation.4 | async-start | bytes 131072 | tf_op jit(solution)/shard_map/psum | solution.py:52
  65.0 8.7 %collective-permute-start.3 = (f32[32,2,1,1024]{3,0,2,1:T(8,128)S(1)}, f32[32,2,1,1024]{3,0,2,1:T(8,128)S(1)}, u32[]{:S(2)}, u32[]{:S(2)}) collective-permute-start(f32[32,2,1,1024]{3,0,2,1:T(8,128)S(1)} %get-tuple-element.49), channel_id=1, source_target_pairs={{0,4},{4,8},{8,12},{12,16},{16,20},{20,24},{24,28},{28,32},{32,36}... | collective-permute-start | bytes 786440 | tf_op jit(solution)/shard_map/ppermute | solution.py:17
  68.2 9.5 %copy-start.17 = (f32[2,8,1024]{2,1,0:T(8,128)S(1)}, f32[2,8,1024]{2,1,0:T(8,128)}, u32[]{:S(2)}) copy-start(f32[2,8,1024]{2,1,0:T(8,128)} %param.16) | copy-start | bytes 196612
  68.3 9.5 %copy-start.22 = (f32[2,8,1024]{2,1,0:T(8,128)S(1)}, f32[2,8,1024]{2,1,0:T(8,128)}, u32[]{:S(2)}) copy-start(f32[2,8,1024]{2,1,0:T(8,128)} %param.14) | copy-start | bytes 196612
  68.3 9.5 %copy-start.24 = (f32[2,8,1024]{2,1,0:T(8,128)S(1)}, f32[2,8,1024]{2,1,0:T(8,128)}, u32[]{:S(2)}) copy-start(f32[2,8,1024]{2,1,0:T(8,128)} %param.15) | copy-start | bytes 196612
  68.3 9.5 %collective-permute-start.2 = (f32[32,2,1,1024]{3,0,2,1:T(8,128)S(1)}, f32[32,2,1,1024]{3,0,2,1:T(8,128)S(1)}, u32[]{:S(2)}, u32[]{:S(2)}) collective-permute-start(f32[32,2,1,1024]{3,0,2,1:T(8,128)S(1)} %get-tuple-element.48), channel_id=1, source_target_pairs={{4,0},{8,4},{12,8},{16,12},{20,16},{24,20},{28,24},{32,28},{36,32}... | collective-permute-start | bytes 786440 | tf_op jit(solution)/shard_map/ppermute | solution.py:18
  69.7 8.1 %copy-start.7 = (f32[32,2,8,1024]{3,2,1,0:T(8,128)S(1)}, f32[32,2,8,1024]{3,2,1,0:T(8,128)}, u32[]{:S(2)}) copy-start(f32[32,2,8,1024]{3,2,1,0:T(8,128)} %param.12) | copy-start | bytes 6291460
  70.5 13.2 %copy-start.5 = (f32[32,2,8,1023]{3,0,2,1:T(8,128)}, f32[32,2,8,1023]{3,0,2,1:T(8,128)S(1)}, u32[]{:S(2)}) copy-start(f32[32,2,8,1023]{3,0,2,1:T(8,128)S(1)} %get-tuple-element.50) | copy-start | bytes 6285316
  70.5 13.2 %copy-start.6 = (f32[32,2,8,1023]{3,0,2,1:T(8,128)}, f32[32,2,8,1023]{3,0,2,1:T(8,128)S(1)}, u32[]{:S(2)}) copy-start(f32[32,2,8,1023]{3,0,2,1:T(8,128)S(1)} %get-tuple-element.51) | copy-start | bytes 6285316
  86.1 56.0 %collective-permute-start.1 = (f32[2,32,2,1,1024]{4,1,3,2,0:T(8,128)}, f32[2,32,2,1,1024]{4,1,3,2,0:T(8,128)}, u32[]{:S(2)}, u32[]{:S(2)}) collective-permute-start(f32[2,32,2,1,1024]{4,1,3,2,0:T(8,128)} %get-tuple-element.28), channel_id=1, source_target_pairs={{4,0},{8,4},{12,8},{16,12},{20,16},{24,20},{28,24},{32,28},{36,32}... | collective-permute-start | bytes 1572872 | tf_op jit(solution)/shard_map/ppermute | solution.py:18
  87.4 54.7 %collective-permute-start = (f32[2,32,2,1,1024]{4,1,3,2,0:T(8,128)}, f32[2,32,2,1,1024]{4,1,3,2,0:T(8,128)}, u32[]{:S(2)}, u32[]{:S(2)}) collective-permute-start(f32[2,32,2,1,1024]{4,1,3,2,0:T(8,128)} %get-tuple-element.27), channel_id=1, source_target_pairs={{0,4},{4,8},{8,12},{12,16},{16,20},{20,24},{24,28},{28,32},{32,36}... | collective-permute-start | bytes 1572872 | tf_op jit(solution)/shard_map/ppermute | solution.py:17
  92.8 108.9 %all-reduce.9.cloned.1.call-start = ((), (), s32[]{:S(2)}) async-start(), calls=%async_computation.5 | async-start | bytes 131072 | tf_op jit(solution)/shard_map/psum | solution.py:95
  157.0 122.7 %all-reduce.11.cloned.1.call-start = ((), (), s32[]{:S(2)}) async-start(), calls=%async_computation.6 | async-start | bytes 131072 | tf_op jit(solution)/shard_map/psum | solution.py:95
  159.0 55.9 %collective-permute-start.6 = (f32[32,2,1,1024]{3,0,2,1:T(8,128)}, f32[32,2,1,1024]{3,0,2,1:T(8,128)}, u32[]{:S(2)}, u32[]{:S(2)}) collective-permute-start(f32[32,2,1,1024]{3,0,2,1:T(8,128)} %get-tuple-element.43), channel_id=1, source_target_pairs={{4,0},{8,4},{12,8},{16,12},{20,16},{24,20},{28,24},{32,28},{36,32}... | collective-permute-start | bytes 786440 | tf_op jit(solution)/shard_map/ppermute | solution.py:18
  160.3 54.6 %collective-permute-start.7 = (f32[32,2,1,1024]{3,0,2,1:T(8,128)}, f32[32,2,1,1024]{3,0,2,1:T(8,128)}, u32[]{:S(2)}, u32[]{:S(2)}) collective-permute-start(f32[32,2,1,1024]{3,0,2,1:T(8,128)} %get-tuple-element.42), channel_id=1, source_target_pairs={{0,4},{4,8},{8,12},{12,16},{16,20},{20,24},{24,28},{28,32},{32,36}... | collective-permute-start | bytes 786440 | tf_op jit(solution)/shard_map/ppermute | solution.py:17
  208.3 6.6 %copy-start.11 = (f32[32,2,8,1023]{3,0,2,1:T(8,128)S(1)}, f32[32,2,8,1023]{3,0,2,1:T(8,128)}, u32[]{:S(2)}) copy-start(f32[32,2,8,1023]{3,0,2,1:T(8,128)} %get-tuple-element.44) | copy-start | bytes 6285316
  208.3 6.6 %copy-start.12 = (f32[32,2,8,1023]{3,0,2,1:T(8,128)S(1)}, f32[32,2,8,1023]{3,0,2,1:T(8,128)}, u32[]{:S(2)}) copy-start(f32[32,2,8,1023]{3,0,2,1:T(8,128)} %get-tuple-element.45) | copy-start | bytes 6285316
  209.0 15.8 %collective-permute-start.5 = (f32[2,32,2,1,1024]{4,1,3,2,0:T(8,128)S(1)}, f32[2,32,2,1,1024]{4,1,3,2,0:T(8,128)S(1)}, u32[]{:S(2)}, u32[]{:S(2)}) collective-permute-start(f32[2,32,2,1,1024]{4,1,3,2,0:T(8,128)S(1)} %get-tuple-element.26), channel_id=1, source_target_pairs={{4,0},{8,4},{12,8},{16,12},{20,16},{24,20},{28,24},{32,28},{36,32}... | collective-permute-start | bytes 1572872 | tf_op jit(solution)/shard_map/ppermute | solution.py:18
  210.5 15.1 %collective-permute-start.4 = (f32[2,32,2,1,1024]{4,1,3,2,0:T(8,128)S(1)}, f32[2,32,2,1,1024]{4,1,3,2,0:T(8,128)S(1)}, u32[]{:S(2)}, u32[]{:S(2)}) collective-permute-start(f32[2,32,2,1,1024]{4,1,3,2,0:T(8,128)S(1)} %get-tuple-element.25), channel_id=1, source_target_pairs={{0,4},{4,8},{8,12},{12,16},{16,20},{20,24},{24,28},{28,32},{32,36}... | collective-permute-start | bytes 1572872 | tf_op jit(solution)/shard_map/ppermute | solution.py:17
  228.1 51.6 %copy-start.33 = (f32[32]{0:T(128)S(1)}, f32[32]{0:T(128)}, u32[]{:S(2)}) copy-start(f32[32]{0:T(128)} %get-tuple-element.56) | copy-start | bytes 388
  231.7 81.1 %reduce-scatter.4.cloned.1.call-start = ((), (), s32[]{:S(2)}) async-start(), calls=%async_computation.7 | async-start | bytes 81920 | tf_op jit(solution)/shard_map/reduce_scatter | solution.py:75
  232.4 114.6 %reduce-scatter.6.cloned.1.call-start = ((), (), s32[]{:S(2)}) async-start(), calls=%async_computation.8 | async-start | bytes 81920 | tf_op jit(solution)/shard_map/reduce_scatter | solution.py:76
  233.2 148.2 %reduce-scatter.8.cloned.1.call-start = ((), (), s32[]{:S(2)}) async-start(), calls=%async_computation.9 | async-start | bytes 81920 | tf_op jit(solution)/shard_map/reduce_scatter | solution.py:77
  (25 other events, 96.1 us)
Sparse Core Ops, SparseCore 0:
  11.8 49.3 all-reduce.4
  93.0 48.2 all-reduce.6
  157.2 44.5 all-reduce.8
  231.8 47.8 all-reduce.10
  282.8 29.9 reduce-scatter.3
  316.0 31.0 reduce-scatter.5
  350.3 31.0 reduce-scatter.7
where the time goes:
time: 389 us; the launch traced here: 388 us
  waiting for transfers between devices  285 us (73%)
  other arithmetic  43 us (11%)
  starting transfers between devices  22.7 us (6%)
  local copies, waits for them, and re-layouts  22.4 us (6%)
  between operations  14.7 us (4%)
    psum x2, waiting for transfers between devices, local(): crowd = lax.psum(jnp.sum(weight * state, axis=0), 'coh') / COH  91 us
    psum x2, waiting for transfers between devices, local(): lax.psum(jnp.sum(-crowding * grad_surv * survived, axis=0), 'coh')  82.6 us
    reduce_scatter x1, waiting for transfers between devices, local(): lax.psum_scatter(grad_kappa, 'coh', scatter_dimension=2, tiled=True)  34.3 us
    reduce_scatter x1, waiting for transfers between devices, local(): lax.psum_scatter(grad_north, 'coh', scatter_dimension=2, tiled=True)  34.2 us
    reduce_scatter x1, waiting for transfers between devices, local(): lax.psum_scatter(grad_east, 'coh', scatter_dimension=2, tiled=True)  29.2 us
    ppermute x4, starting transfers between devices, extended(): before = lax.ppermute(last, axis, up)  16.8 us
    reduce_sum x2, other arithmetic, local(): grad_kappa = jnp.sum(masked * laplace, axis=0)  9.98 us
    ppermute x4, waiting for transfers between devices, extended(): after = lax.ppermute(first, axis, down)  9.14 us
  transfers between devices with their start and end apart: 15, of which 11 were waited for; matrix products, arithmetic and copies ran while one was open for 7% of the time, Pallas kernels for 0%

commit v1 on v0

--- a/solution.py
+++ b/solution.py
@@ -5,6 +5,11 @@
 
 COH = 128
 STEPS = 2
+
+
+def gather_and_add(value, axis):
+    parts = lax.all_gather(value, axis)
+    return jnp.sum(parts, axis=0)
 
 
 def extended(value, sides, width):
@@ -49,7 +54,7 @@
     state = density
     saved = []
     for section in range(STEPS):
-        crowd = lax.psum(jnp.sum(weight * state, axis=0), "coh") / COH
+        crowd = gather_and_add(jnp.sum(weight * state, axis=0), "coh") / COH
         survival = jnp.exp(-(mortal + crowding * crowd[None]))
         survived = state * survival
         wet = ocean * survived

time: 389 us -> 322 us (0.83)
  waiting for transfers between devices: 285 us -> 203 us
  blocking collectives: 0 us -> 19.4 us
    psum x2 -> x0, waiting for transfers between devices: 91 us -> none  [local(): crowd = lax.psum(jnp.sum(weight * state, axis=0), 'coh') / COH]
    all_gather x0 -> x2, blocking collectives: none -> 19.4 us  [gather_and_add(): parts = lax.all_gather(value, axis)]
    psum x2, waiting for transfers between devices: 82.6 us -> 92.5 us  [local(): lax.psum(jnp.sum(-crowding * grad_surv * survived, axis=0), 'coh')]
  transfers between devices with their start and end apart: 15 -> 13, of which waited for: 11 -> 9; matrix products, arithmetic and copies ran while one was open for 7% -> 8% of each run, Pallas kernels for 0% -> 0%
where the time goes in v1:
time: 322 us; the launch traced here: 321 us
  waiting for transfers between devices  203 us (63%)
  other arithmetic  42.2 us (13%)
  starting transfers between devices  22.1 us (7%)
  blocking collectives  19.4 us (6%)
  local copies, waits for them, and re-layouts  19.1 us (6%)
  between operations  14.3 us (4%)
    psum x2, waiting for transfers between devices, local(): lax.psum(jnp.sum(-crowding * grad_surv * survived, axis=0), 'coh')  92.5 us
    reduce_scatter x1, waiting for transfers between devices, local(): lax.psum_scatter(grad_north, 'coh', scatter_dimension=2, tiled=True)  34.2 us
    reduce_scatter x1, waiting for transfers between devices, local(): lax.psum_scatter(grad_kappa, 'coh', scatter_dimension=2, tiled=True)  34.2 us
    reduce_scatter x1, waiting for transfers between devices, local(): lax.psum_scatter(grad_east, 'coh', scatter_dimension=2, tiled=True)  29.3 us
    all_gather x2, blocking collectives, gather_and_add(): parts = lax.all_gather(value, axis)  19.4 us
    ppermute x4, starting transfers between devices, extended(): before = lax.ppermute(last, axis, up)  16.4 us
    reduce_sum x2, other arithmetic, local(): grad_kappa = jnp.sum(masked * laplace, axis=0)  9.92 us
    ppermute x4, waiting for transfers between devices, extended(): after = lax.ppermute(first, axis, down)  9.5 us
  transfers between devices with their start and end apart: 13, of which 9 were waited for; matrix products, arithmetic and copies ran while one was open for 8% of the time, Pallas kernels for 0%

profile of v1, /device:TPU:1, one launch (start us, length us, event | category | flops | bytes accessed | tf_op | source)
XLA Modules:
  0.0 321.1 jit_solution(662250210040617315)
XLA Ops:
  8.1 2.8 multiply_reduce_fusion.9
  11.0 10.3 %all-gather = f32[8,8,1024]{2,1,0:T(8,128)S(1)} all-gather(f32[2,8,1024]{2,1,0:T(8,128)S(1)} %multiply_reduce_fusion.9), channel_id=2, replica_groups=mesh['lat'=64,'coh'=4] {'coh'}, dimensions={0}, use_global_device_ids=true | all-gather | bytes 327680 | tf_op jit(solution)/shard_map/all_gather | solution.py:11
  21.4 3.0 fusion.26
  24.4 2.0 collective-permute-start.3
  29.5 2.4 collective-permute-done.3
  31.9 4.4 %collective-permute-done.2 = f32[32,2,1,1024]{3,0,2,1:T(8,128)S(1)} collective-permute-done((f32[32,2,1,1024]{3,0,2,1:T(8,128)S(1)}, f32[32,2,1,1024]{3,0,2,1:T(8,128)S(1)}, u32[]{:S(2)}, u32[]{:S(2)}) %collective-permute-start.2) | collective-permute-done | bytes 262176 | tf_op jit(solution)/shard_map/ppermute | solution.py:23
  36.2 5.0 %fusion.9 = (f32[32,2,8,1024]{3,0,2,1:T(8,128)}, f32[32,2,8,1024]{3,0,2,1:T(8,128)S(1)}, f32[1,32,2,8,1024]{4,1,3,2,0:T(8,128)S(1)}, f32[1,32,2,8,1024]{4,1,3,2,...) fusion(f32[2,8,1024]{2,1,0:T(8,128)S(1)} %copy-done.21, f32[32]{0:T(128)S(1)} %get-tuple-element.58, ...), kind=kLoop, calls=%fused_computation.15 | loop fusion | flops 18333696 | bytes 19726592 | tf_op jit(solution)/shard_map/mul | solution.py:87
  44.9 5.0 %collective-permute-start = (f32[2,32,2,1,1024]{4,1,3,2,0:T(8,128)}, f32[2,32,2,1,1024]{4,1,3,2,0:T(8,128)}, u32[]{:S(2)}, u32[]{:S(2)}) collective-permute-start(f32[2,32,2,1,1024]{4,1,3,2,0:T(8,128)} %get-tuple-element.27), channel_id=1, source_target_pairs={{0,4},{4,8},{8,12},{12,16},{16,20},{20,24},{24,28},{28,32},{32,36}... | collective-permute-start | bytes 1572872 | tf_op jit(solution)/shard_map/ppermute | solution.py:22
  52.4 9.0 %all-gather.1 = f32[8,8,1024]{2,1,0:T(8,128)} all-gather(f32[2,8,1024]{2,1,0:T(8,128)S(1)} %get-tuple-element.54), channel_id=3, replica_groups=mesh['lat'=64,'coh'=4] {'coh'}, dimensions={0}, use_global_device_ids=true | all-gather | bytes 327680 | tf_op jit(solution)/shard_map/all_gather | solution.py:11
  65.0 3.1 pad_maximum_fusion
  71.6 4.5 %multiply_reduce_fusion.7 = (f32[2,8,1024]{2,1,0:T(8,128)}, f32[32,2,8,1024]{3,0,2,1:T(8,128)}, f32[32,2,8,1024]{3,0,2,1:T(8,128)S(1)}) fusion(f32[32,2,8,1024]{3,0,2,1:T(8,128)S(1)} %copy-done.13, f32[32]{0:T(128)S(1)} %get-tuple-element.57, f32[2,8,1024]{2,1,0:T(8,128)S(1)} %broadcast_multiply_fusion, f32[32]{0:T(128)S(1)} %get-tuple-element.60, ...), kind=kLoop, calls=%fused_computation.57 | loop fusion | flops 8896512 | bytes 17039744 | tf_op jit(solution)/shard_map/reduce_sum | solution.py:100
  76.1 2.9 fusion.42
  83.0 5.2 %collective-permute-start.7 = (f32[32,2,1,1024]{3,0,2,1:T(8,128)}, f32[32,2,1,1024]{3,0,2,1:T(8,128)}, u32[]{:S(2)}, u32[]{:S(2)}) collective-permute-start(f32[32,2,1,1024]{3,0,2,1:T(8,128)} %get-tuple-element.42), channel_id=1, source_target_pairs={{0,4},{4,8},{8,12},{12,16},{16,20},{20,24},{24,28},{28,32},{32,36}... | collective-permute-start | bytes 786440 | tf_op jit(solution)/shard_map/ppermute | solution.py:22
  88.3 46.6 %all-reduce.3.cloned.1.call-done = f32[2,8,1024]{2,1,0:T(8,128)} async-done(((f32[2,8,1024]{2,1,0:T(8,128)}), f32[2,8,1024]{2,1,0:T(8,128)}) %all-reduce.3.cloned.1.call-update) | async-done | bytes 65552 | tf_op jit(solution)/shard_map/psum | solution.py:100
  134.9 5.2 %multiply_reduce_fusion = (f32[2,8,1024]{2,1,0:T(8,128)}, f32[2,8,1024]{2,1,0:T(8,128)}, f32[2,8,1024]{2,1,0:T(8,128)}, f32[32,2,8,1024]{3,0,2,1:T(8,128)S(1)}) fusion(f32[32,2,8,1024]{3,0,2,1:T(8,128)S(1)} %fusion.26, f32[32,2,8,1023]{3,0,2,1:T(8,128)} %copy-done.6, f32[32,2,8,1]{3,0,2,1:T(8,128)S(1)} %get-tuple-element.53, ...), kind=kLoop, calls=%fused_computation.48 | loop fusion | flops 14106624 | bytes 11403776 | tf_op jit(solution)/shard_map/reduce_sum | solution.py:78
  143.7 4.2 %collective-permute-start.4 = (f32[2,32,2,1,1024]{4,1,3,2,0:T(8,128)S(1)}, f32[2,32,2,1,1024]{4,1,3,2,0:T(8,128)S(1)}, u32[]{:S(2)}, u32[]{:S(2)}) collective-permute-start(f32[2,32,2,1,1024]{4,1,3,2,0:T(8,128)S(1)} %get-tuple-element.25), channel_id=1, source_target_pairs={{0,4},{4,8},{8,12},{12,16},{16,20},{20,24},{24,28},{28,32},{32,36}... | collective-permute-start | bytes 1572872 | tf_op jit(solution)/shard_map/ppermute | solution.py:22
  148.1 4.7 %multiply_reduce_fusion.1 = (f32[2,8,1024]{2,1,0:T(8,128)}, f32[2,8,1024]{2,1,0:T(8,128)}, f32[2,8,1024]{2,1,0:T(8,128)}) fusion(f32[32,2,8,1024]{3,0,2,1:T(8,128)S(1)} %copy-done.1, f32[32,2,8,1023]{3,0,2,1:T(8,128)S(1)} %copy-done.12, f32[32,2,8,1]{3,0,2,1:T(8,128)S(1)} %copy-done.15, f32[32,2,8,1]{3,0,2,1:T(8,128)S(1)} %get-tuple-element.46, ...), kind=kLoop, calls=%fused_computation.49 | loop fusion | flops 10960896 | bytes 9175168 | tf_op jit(solution)/shard_map/reduce_sum | solution.py:78
  152.8 5.1 %collective-permute-done.5 = f32[2,32,2,1,1024]{4,1,3,2,0:T(8,128)S(1)} collective-permute-done((f32[2,32,2,1,1024]{4,1,3,2,0:T(8,128)S(1)}, f32[2,32,2,1,1024]{4,1,3,2,0:T(8,128)S(1)}, u32[]{:S(2)}, u32[]{:S(2)}) %collective-permute-start.5) | collective-permute-done | bytes 524320 | tf_op jit(solution)/shard_map/ppermute | solution.py:23
  161.3 3.6 %multiply_reduce_fusion.6 = (f32[2,8,1024]{2,1,0:T(8,128)}, f32[32,2,8,1024]{3,0,2,1:T(8,128)S(1)}) fusion(f32[32,2,8,1024]{3,2,1,0:T(8,128)S(1)} %copy-done.2, f32[32]{0:T(128)S(1)} %get-tuple-element.57, f32[2,8,1024]{2,1,0:T(8,128)S(1)} %broadcast_multiply_fusion.1, f32[32]{0:T(128)S(1)} %get-tuple-element.60, f32[32]{0:T(128)S(1)} %get-tuple-element.61, ...), kind=kLoop, calls=%fused_computation.55 | loop fusion | flops 7847936 | bytes 14942592 | tf_op jit(solution)/shard_map/reduce_sum | solution.py:100
  167.0 45.8 %all-reduce.5.cloned.1.call-done = f32[2,8,1024]{2,1,0:T(8,128)} async-done(((f32[2,8,1024]{2,1,0:T(8,128)}), f32[2,8,1024]{2,1,0:T(8,128)}) %all-reduce.5.cloned.1.call-update) | async-done | bytes 65552 | tf_op jit(solution)/shard_map/psum | solution.py:100
  214.3 2.5 copy.18
  216.8 29.3 %reduce-scatter.4.cloned.1.call-done = f32[2,8,256]{2,1,0:T(8,128)} async-done(((f32[2,8,1024]{2,1,0:T(8,128)}), f32[2,8,256]{2,1,0:T(8,128)}) %reduce-scatter.4.cloned.1.call-update) | async-done | bytes 16400 | tf_op jit(solution)/shard_map/reduce_scatter | solution.py:80
  246.2 34.2 %reduce-scatter.6.cloned.1.call-done = f32[2,8,256]{2,1,0:T(8,128)} async-done(((f32[2,8,1024]{2,1,0:T(8,128)}), f32[2,8,256]{2,1,0:T(8,128)}) %reduce-scatter.6.cloned.1.call-update) | async-done | bytes 16400 | tf_op jit(solution)/shard_map/reduce_scatter | solution.py:81
  280.4 34.2 %reduce-scatter.8.cloned.1.call-done = f32[2,8,256]{2,1,0:T(8,128)} async-done(((f32[2,8,1024]{2,1,0:T(8,128)}), f32[2,8,256]{2,1,0:T(8,128)}) %reduce-scatter.8.cloned.1.call-update) | async-done | bytes 16400 | tf_op jit(solution)/shard_map/reduce_scatter | solution.py:82
  (115 shorter events, 31.6 us)
Async XLA Ops:
  7.2 14.2 %copy-start.31 = (s32[2,8,1024]{2,1,0:T(8,128)S(1)}, s32[2,8,1024]{2,1,0:T(8,128)}, u32[]{:S(2)}) copy-start(s32[2,8,1024]{2,1,0:T(8,128)} %param.13) | copy-start | bytes 196612
  7.2 127.7 %all-reduce.3.cloned.1.call-start = ((), (), s32[]{:S(2)}) async-start(), calls=%async_computation.3 | async-start | bytes 131072 | tf_op jit(solution)/shard_map/psum | solution.py:100
  24.4 7.5 %collective-permute-start.3 = (f32[32,2,1,1024]{3,0,2,1:T(8,128)S(1)}, f32[32,2,1,1024]{3,0,2,1:T(8,128)S(1)}, u32[]{:S(2)}, u32[]{:S(2)}) collective-permute-start(f32[32,2,1,1024]{3,0,2,1:T(8,128)S(1)} %get-tuple-element.49), channel_id=1, source_target_pairs={{0,4},{4,8},{8,12},{12,16},{16,20},{20,24},{24,28},{28,32},{32,36}... | collective-permute-start | bytes 786440 | tf_op jit(solution)/shard_map/ppermute | solution.py:22
  26.4 9.8 %copy-start.21 = (f32[2,8,1024]{2,1,0:T(8,128)S(1)}, f32[2,8,1024]{2,1,0:T(8,128)}, u32[]{:S(2)}) copy-start(f32[2,8,1024]{2,1,0:T(8,128)} %param.14) | copy-start | bytes 196612
  26.4 9.8 %copy-start.23 = (f32[2,8,1024]{2,1,0:T(8,128)S(1)}, f32[2,8,1024]{2,1,0:T(8,128)}, u32[]{:S(2)}) copy-start(f32[2,8,1024]{2,1,0:T(8,128)} %param.15) | copy-start | bytes 196612
  26.4 9.8 %collective-permute-start.2 = (f32[32,2,1,1024]{3,0,2,1:T(8,128)S(1)}, f32[32,2,1,1024]{3,0,2,1:T(8,128)S(1)}, u32[]{:S(2)}, u32[]{:S(2)}) collective-permute-start(f32[32,2,1,1024]{3,0,2,1:T(8,128)S(1)} %get-tuple-element.48), channel_id=1, source_target_pairs={{4,0},{8,4},{12,8},{16,12},{20,16},{24,20},{28,24},{32,28},{36,32}... | collective-permute-start | bytes 786440 | tf_op jit(solution)/shard_map/ppermute | solution.py:23
  27.9 8.4 %copy-start.7 = (f32[32,2,8,1024]{3,2,1,0:T(8,128)S(1)}, f32[32,2,8,1024]{3,2,1,0:T(8,128)}, u32[]{:S(2)}) copy-start(f32[32,2,8,1024]{3,2,1,0:T(8,128)} %param.12) | copy-start | bytes 6291460
  28.6 12.6 %copy-start.5 = (f32[32,2,8,1023]{3,0,2,1:T(8,128)}, f32[32,2,8,1023]{3,0,2,1:T(8,128)S(1)}, u32[]{:S(2)}) copy-start(f32[32,2,8,1023]{3,0,2,1:T(8,128)S(1)} %get-tuple-element.50) | copy-start | bytes 6285316
  28.7 12.6 %copy-start.6 = (f32[32,2,8,1023]{3,0,2,1:T(8,128)}, f32[32,2,8,1023]{3,0,2,1:T(8,128)S(1)}, u32[]{:S(2)}) copy-start(f32[32,2,8,1023]{3,0,2,1:T(8,128)S(1)} %get-tuple-element.51) | copy-start | bytes 6285316
  43.6 21.3 %collective-permute-start.1 = (f32[2,32,2,1,1024]{4,1,3,2,0:T(8,128)}, f32[2,32,2,1,1024]{4,1,3,2,0:T(8,128)}, u32[]{:S(2)}, u32[]{:S(2)}) collective-permute-start(f32[2,32,2,1,1024]{4,1,3,2,0:T(8,128)} %get-tuple-element.28), channel_id=1, source_target_pairs={{4,0},{8,4},{12,8},{16,12},{20,16},{24,20},{28,24},{32,28},{36,32}... | collective-permute-start | bytes 1572872 | tf_op jit(solution)/shard_map/ppermute | solution.py:23
  44.9 20.1 %collective-permute-start = (f32[2,32,2,1,1024]{4,1,3,2,0:T(8,128)}, f32[2,32,2,1,1024]{4,1,3,2,0:T(8,128)}, u32[]{:S(2)}, u32[]{:S(2)}) collective-permute-start(f32[2,32,2,1,1024]{4,1,3,2,0:T(8,128)} %get-tuple-element.27), channel_id=1, source_target_pairs={{0,4},{4,8},{8,12},{12,16},{16,20},{20,24},{24,28},{28,32},{32,36}... | collective-permute-start | bytes 1572872 | tf_op jit(solution)/shard_map/ppermute | solution.py:22
  79.8 133.1 %all-reduce.5.cloned.1.call-start = ((), (), s32[]{:S(2)}) async-start(), calls=%async_computation.4 | async-start | bytes 131072 | tf_op jit(solution)/shard_map/psum | solution.py:100
  81.7 66.3 %collective-permute-start.6 = (f32[32,2,1,1024]{3,0,2,1:T(8,128)}, f32[32,2,1,1024]{3,0,2,1:T(8,128)}, u32[]{:S(2)}, u32[]{:S(2)}) collective-permute-start(f32[32,2,1,1024]{3,0,2,1:T(8,128)} %get-tuple-element.43), channel_id=1, source_target_pairs={{4,0},{8,4},{12,8},{16,12},{20,16},{24,20},{28,24},{32,28},{36,32}... | collective-permute-start | bytes 786440 | tf_op jit(solution)/shard_map/ppermute | solution.py:23
  83.0 65.0 %collective-permute-start.7 = (f32[32,2,1,1024]{3,0,2,1:T(8,128)}, f32[32,2,1,1024]{3,0,2,1:T(8,128)}, u32[]{:S(2)}, u32[]{:S(2)}) collective-permute-start(f32[32,2,1,1024]{3,0,2,1:T(8,128)} %get-tuple-element.42), channel_id=1, source_target_pairs={{0,4},{4,8},{8,12},{12,16},{16,20},{20,24},{24,28},{28,32},{32,36}... | collective-permute-start | bytes 786440 | tf_op jit(solution)/shard_map/ppermute | solution.py:22
  141.4 6.6 %copy-start.11 = (f32[32,2,8,1023]{3,0,2,1:T(8,128)S(1)}, f32[32,2,8,1023]{3,0,2,1:T(8,128)}, u32[]{:S(2)}) copy-start(f32[32,2,8,1023]{3,0,2,1:T(8,128)} %get-tuple-element.44) | copy-start | bytes 6285316
  141.4 6.6 %copy-start.12 = (f32[32,2,8,1023]{3,0,2,1:T(8,128)S(1)}, f32[32,2,8,1023]{3,0,2,1:T(8,128)}, u32[]{:S(2)}) copy-start(f32[32,2,8,1023]{3,0,2,1:T(8,128)} %get-tuple-element.45) | copy-start | bytes 6285316
  142.0 6.0 %copy-start.1 = (f32[32,2,8,1024]{3,0,2,1:T(8,128)S(1)}, f32[32,2,8,1024]{3,0,2,1:T(8,128)}, u32[]{:S(2)}) copy-start(f32[32,2,8,1024]{3,0,2,1:T(8,128)} %copy-done) | copy-start | bytes 6291460
  142.0 6.0 %copy-start.9 = (f32[32,2,8,1024]{3,2,1,0:T(8,128)S(1)}, f32[32,2,8,1024]{3,2,1,0:T(8,128)}, u32[]{:S(2)}) copy-start(f32[32,2,8,1024]{3,2,1,0:T(8,128)} %param.12) | copy-start | bytes 6291460
  142.1 15.8 %collective-permute-start.5 = (f32[2,32,2,1,1024]{4,1,3,2,0:T(8,128)S(1)}, f32[2,32,2,1,1024]{4,1,3,2,0:T(8,128)S(1)}, u32[]{:S(2)}, u32[]{:S(2)}) collective-permute-start(f32[2,32,2,1,1024]{4,1,3,2,0:T(8,128)S(1)} %get-tuple-element.26), channel_id=1, source_target_pairs={{4,0},{8,4},{12,8},{16,12},{20,16},{24,20},{28,24},{32,28},{36,32}... | collective-permute-start | bytes 1572872 | tf_op jit(solution)/shard_map/ppermute | solution.py:23
  143.7 15.1 %collective-permute-start.4 = (f32[2,32,2,1,1024]{4,1,3,2,0:T(8,128)S(1)}, f32[2,32,2,1,1024]{4,1,3,2,0:T(8,128)S(1)}, u32[]{:S(2)}, u32[]{:S(2)}) collective-permute-start(f32[2,32,2,1,1024]{4,1,3,2,0:T(8,128)S(1)} %get-tuple-element.25), channel_id=1, source_target_pairs={{0,4},{4,8},{8,12},{12,16},{16,20},{20,24},{24,28},{28,32},{32,36}... | collective-permute-start | bytes 1572872 | tf_op jit(solution)/shard_map/ppermute | solution.py:22
  161.3 51.6 %copy-start.32 = (f32[32]{0:T(128)S(1)}, f32[32]{0:T(128)}, u32[]{:S(2)}) copy-start(f32[32]{0:T(128)} %get-tuple-element.56) | copy-start | bytes 388
  164.9 81.3 %reduce-scatter.4.cloned.1.call-start = ((), (), s32[]{:S(2)}) async-start(), calls=%async_computation.5 | async-start | bytes 81920 | tf_op jit(solution)/shard_map/reduce_scatter | solution.py:80
  165.6 114.7 %reduce-scatter.6.cloned.1.call-start = ((), (), s32[]{:S(2)}) async-start(), calls=%async_computation.6 | async-start | bytes 81920 | tf_op jit(solution)/shard_map/reduce_scatter | solution.py:81
  166.3 148.2 %reduce-scatter.8.cloned.1.call-start = ((), (), s32[]{:S(2)}) async-start(), calls=%async_computation.7 | async-start | bytes 81920 | tf_op jit(solution)/shard_map/reduce_scatter | solution.py:82
  (22 other events, 78.2 us)
Sparse Core Ops, SparseCore 0:
  79.9 54.9 all-reduce.2
  165.0 47.8 all-reduce.4
  216.1 29.9 reduce-scatter.3
  249.3 31.0 reduce-scatter.5
  283.4 31.0 reduce-scatter.7
